TPU v7x, 512 devices: a whole 4x4x16 slice. The times are simulated.
512 devices in a mesh: dp: 64 (over x, z), ctx: 8 (over y, core).
Axes of the slice: x: 4, y: 4, z: 16, core: 2. Of those that a mesh axis runs over, the one named last changes fastest.
Arguments:
- projections: bfloat16 [131072, 6144], P(('dp', 'ctx')), may hold values from -6 to 6
- block_source: int32 [64, 8, 2], P('dp', 'ctx'), may hold values from 0 to 1023, as said below
- clip_ids: int32 [64, 16], P('dp'), may hold values from 0 to 8, as said below
- out_weight: bfloat16 [2048, 1536], P('dp'), may hold values from -1 to 1
Outputs:
- mixed: bfloat16 [131072, 1536], P(('dp', 'ctx'))
Inputs may be any that keep to these rules, and one draw needn't show every extreme that they name: `block_source`: arrival block a lies on the device numbered a // 2 in dp-major order (dp index a // (2 * 8), ctx index (a // 2) % 8). The block that fills pack block (o, j, l) lies on the device with the same ctx index j and dp index o or o XOR 1. Every arrival block fills exactly one pack block. `clip_ids`: in each pack the clip numbers start at 0, never fall and rise by at most one from block to block; every clip spans 1 to 8 blocks, and in every pack some clip spans exactly 8 blocks.
All inputs are finite; a program needn't handle non-finite values.
Results may differ from a plain program's by a relative error of at most 0.0057.
Values may be sent and summed in bfloat16 or wider, within the bound.
A program may use at most 64 MiB of HBM per device.

v0:
```python
import math
import jax
import jax.numpy as jnp
from jax import lax
from jax.sharding import PartitionSpec as P

HEAD = 128
big_negative = -1e30


def partner(value, axis, bit):
    mask = 2**bit
    pairs = [(source, source ^ mask) for source in range(lax.axis_size(axis))]
    return lax.ppermute(value, axis, pairs)


def soft_weights(scores, allowed):
    masked = jnp.where(allowed, scores, big_negative)
    row_max = jnp.max(masked, axis=-1, keepdims=True)
    exponent = jnp.exp(masked - row_max)
    return (exponent / jnp.sum(exponent, axis=-1, keepdims=True)).astype(jnp.bfloat16)


def attend_dense(queries, key_rows, value_rows, token_clip, scaling):
    token_count, head_count, head_size = queries.shape
    step_size = min(token_count, 512)
    step_count = token_count // step_size
    query_steps = queries.reshape(step_count, step_size, head_count, head_size)
    clip_steps = token_clip.reshape(step_count, step_size)

    def one_step(arguments):
        query_block, clip_block = arguments
        scores = (
            jnp.einsum("qhe,khe->hqk", query_block, key_rows, preferred_element_type=jnp.float32)
            * scaling
        )
        allowed = (clip_block[:, None] == token_clip[None, :])[None]
        weights = soft_weights(scores, allowed)
        return jnp.einsum(
            "hqk,khe->qhe", weights, value_rows, preferred_element_type=jnp.float32
        ).astype(jnp.bfloat16)

    outputs = lax.map(one_step, (query_steps, clip_steps))
    return outputs.reshape(token_count, head_count, head_size)


def body(projections, block_source, clip_ids, out_weight):
    ctx_count = lax.axis_size("ctx")
    local_rows, row_width = projections.shape
    local_blocks = block_source.shape[2]
    block_rows = local_rows // local_blocks
    own_blocks = projections.reshape(local_blocks, block_rows, row_width)
    partner_blocks = partner(own_blocks, "dp", 0)
    source_ids = block_source.reshape(local_blocks)
    from_partner = source_ids // (local_blocks * ctx_count) != lax.axis_index("dp")
    chosen_slot = source_ids % local_blocks + local_blocks * from_partner.astype(jnp.int32)
    candidates = jnp.concatenate([own_blocks, partner_blocks], axis=0)
    packed = jnp.take(candidates, chosen_slot, axis=0)
    local_heads = row_width // (3 * HEAD) // ctx_count
    grouped = packed.reshape(local_rows, ctx_count, local_heads, 3 * HEAD)
    block_clip = clip_ids.reshape(-1)
    token_clip = jnp.repeat(block_clip, block_rows)
    scaling = 1.0 / math.sqrt(HEAD)
    regrouped = lax.all_to_all(grouped, "ctx", split_axis=1, concat_axis=0, tiled=True)
    token_count = regrouped.shape[0]
    item_count = regrouped.shape[2]
    features = regrouped.reshape(token_count, item_count, 3 * HEAD)
    queries = features[:, :, :HEAD]
    key_rows = features[:, :, HEAD : 2 * HEAD]
    value_rows = features[:, :, 2 * HEAD :]
    attended = attend_dense(queries, key_rows, value_rows, token_clip, scaling)
    merged = attended.reshape(local_rows * ctx_count, local_heads * HEAD)
    attention_rows = lax.all_to_all(merged, "ctx", split_axis=0, concat_axis=1, tiled=True)
    result = jnp.dot(
        attention_rows,
        lax.all_gather(out_weight, "dp", axis=0, tiled=True),
        preferred_element_type=jnp.float32,
    )
    return result.astype(jnp.bfloat16)


def solution(mesh):
    return jax.shard_map(
        body,
        mesh=mesh,
        in_specs=(P(("dp", "ctx"), None), P("dp", "ctx", None), P("dp", None), P("dp", None)),
        out_specs=P(("dp", "ctx"), None),
        check_vma=False,
    )
```

profile of v0, /device:TPU:8, one launch (start us, length us, event | category | flops | bytes accessed | tf_op | source)
XLA Modules:
  0.0 276.1 jit_solution(7214846663131477792)
XLA Ops:
  6.5 3.8 %collective-permute-start = (bf16[2,128,6144]{2,1,0:T(8,128)(2,1)}, bf16[2,128,6144]{2,1,0:T(8,128)(2,1)S(1)}, u32[]{:S(2)}, u32[]{:S(2)}) collective-permute-start(bf16[2,128,6144]{2,1,0:T(8,128)(2,1)} %bitcast.87), channel_id=1, source_target_pairs={{0,8},{8,0},{16,24},{24,16},{32,40},{40,32},{48,56},{56,48},{64,72... | collective-permute-start | bytes 9437192 | tf_op jit(solution)/shard_map/ppermute | solution.py:14
  11.8 66.9 %collective-permute-done = bf16[2,128,6144]{2,1,0:T(8,128)(2,1)S(1)} collective-permute-done((bf16[2,128,6144]{2,1,0:T(8,128)(2,1)}, bf16[2,128,6144]{2,1,0:T(8,128)(2,1)S(1)}, u32[]{:S(2)}, u32[]{:S(2)}) %collective-permute-start) | collective-permute-done | bytes 3145760 | tf_op jit(solution)/shard_map/ppermute | solution.py:14
  78.7 5.1 %pad_maximum_fusion = bf16[4,128,6144]{2,1,0:T(8,128)(2,1)} fusion(bf16[2,128,6144]{2,1,0:T(8,128)(2,1)S(1)} %collective-permute-done, bf16[2,128,6144]{2,1,0:T(8,128)(2,1)} %bitcast.88), kind=kLoop, calls=%fused_computation.27 | loop fusion | flops 3145728 | bytes 12582912 | tf_op jit(solution)/shard_map/concatenate | solution.py:57
  83.7 3.5 %gather_fusion = bf16[2,128,6144]{2,1,0:T(8,128)(2,1)S(1)} fusion(bf16[4,128,6144]{2,1,0:T(8,128)(2,1)} %pad_maximum_fusion, s32[1024]{0:T(1024)S(1)} %pad_clamp_fusion), kind=kCustom, calls=%fused_computation | custom fusion | bytes 6291464 | tf_op jit(solution)/shard_map/jit(_take)/gather | solution.py:58
  87.3 3.5 %gather.7 = bf16[256,8,2,384]{3,2,1,0:T(2,128)(2,1)} reshape(bf16[2,128,6144]{2,1,0:T(8,128)(2,1)S(1)} %gather_fusion) | data formatting | bytes 6291456 | tf_op jit(solution)/shard_map/jit(_take)/gather | solution.py:58
  90.8 5.0 %broadcast_select_fusion = bf16[256,8,2,384]{3,2,1,0:T(2,128)(2,1)S(1)} fusion(bf16[256,8,2,384]{3,2,1,0:T(2,128)(2,1)} %gather.7, pred[256]{0:T(512)(128)(4,1)S(1)} %broadcast_bitcast_fusion.2), kind=kLoop, calls=%fused_computation.28 | loop fusion | flops 1572864 | bytes 6291712 | tf_op jit(solution)/shard_map/jit(_take)/select_n | solution.py:58
  95.8 4.1 %copy.12 = bf16[256,8,2,384]{3,2,0,1:T(2,128)(2,1)} copy(bf16[256,8,2,384]{3,2,1,0:T(2,128)(2,1)S(1)} %broadcast_select_fusion) | data formatting | bytes 6291456 | tf_op jit(solution)/shard_map/jit(_take)/select_n | solution.py:58
  99.9 5.0 %all-to-all-start = ((bf16[256,8,2,384]{3,2,0,1:T(2,128)(2,1)}), bf16[256,8,2,384]{3,2,0,1:T(2,128)(2,1)S(1)}, u32[]{:S(2)}, u32[]{:S(2)}) async-start(bf16[256,8,2,384]{3,2,0,1:T(2,128)(2,1)} %copy.12), calls=%async_computation | async-start | bytes 6291456 | tf_op jit(solution)/shard_map/all_to_all | solution.py:64
  104.9 0.7 all-gather.2.cloned.1.call-update
  106.9 35.0 %all-to-all-done = bf16[256,8,2,384]{3,2,0,1:T(2,128)(2,1)S(1)} async-done(((bf16[256,8,2,384]{3,2,0,1:T(2,128)(2,1)}), bf16[256,8,2,384]{3,2,0,1:T(2,128)(2,1)S(1)}, u32[]{:S(2)}, u32[]{:S(2)}) %all-to-all-start) | async-done | bytes 3145760 | tf_op jit(solution)/shard_map/all_to_all | solution.py:64
  142.5 1.9 fusion.37
  144.3 53.7 %while.11 = (s32[]{:T(128)}, bf16[4,512,2,128]{3,2,1,0:T(2,128)(2,1)S(1)}, s32[4,512]{1,0:T(4,128)S(1)}, bf16[4,512,2,128]{3,1,0,2:T(8,128)(2,1)}, bf16[2048,2,1...) while((s32[]{:T(128)}, ...), condition=%wide.region_3.4_spmd.clone, body=%wide.region_0.3_spmd.clone.sunk | while | flops 1087506432 | bytes 22051484 | solution.py:43
  145.1 7.7 %fusion.51 = (f32[2,512]{1,0:T(2,128)S(1)}, f32[2,512,2048]{2,1,0:T(8,128)}) fusion(pred[512,2048]{1,0:T(8,128)(4,1)S(1)} %broadcast_compare_fusion.2, bf16[2048,2,128]{2,0,1:T(8,128)(2,1)} %get-tuple-element.167, bf16[4,512,2,128]{3,1,0,2:T(8,128)(2,1)} %get-tuple-element.166, s32[]{:T(128)} %get-tuple-element.155), kind=kOutput, calls=%fused_computation.56.clone.1 | convolution fusion | flops 545261568 | bytes 10752512 | tf_op jit(solution)/shard_map/while/body/eval_jaxpr/sub | solution.py:20
  152.7 4.7 %fusion.52 = bf16[1,512,2,128]{3,1,2,0:T(8,128)(2,1)S(1)} fusion(bf16[2048,2,128]{2,0,1:T(8,128)(2,1)S(1)} %get-tuple-element.168, f32[2,512,2048]{2,1,0:T(8,128)} %get-tuple-element.145, f32[2,512]{1,0:T(2,128)S(1)} %get-tuple-element.146), kind=kOutput, calls=%fused_computation.13.clone.1 | convolution fusion | flops 541196288 | bytes 9703424 | tf_op jit(solution)/shard_map/while/body/eval_jaxpr/hqk,khe->qhe/dot_general | solution.py:39
  158.5 7.7 %fusion.51 = (f32[2,512]{1,0:T(2,128)S(1)}, f32[2,512,2048]{2,1,0:T(8,128)}) fusion(pred[512,2048]{1,0:T(8,128)(4,1)S(1)} %broadcast_compare_fusion.2, bf16[2048,2,128]{2,0,1:T(8,128)(2,1)} %get-tuple-element.167, bf16[4,512,2,128]{3,1,0,2:T(8,128)(2,1)} %get-tuple-element.166, s32[]{:T(128)} %get-tuple-element.155), kind=kOutput, calls=%fused_computation.56.clone.1 | convolution fusion | flops 545261568 | bytes 10752512 | tf_op jit(solution)/shard_map/while/body/eval_jaxpr/sub | solution.py:20
  166.2 4.7 %fusion.52 = bf16[1,512,2,128]{3,1,2,0:T(8,128)(2,1)S(1)} fusion(bf16[2048,2,128]{2,0,1:T(8,128)(2,1)S(1)} %get-tuple-element.168, f32[2,512,2048]{2,1,0:T(8,128)} %get-tuple-element.145, f32[2,512]{1,0:T(2,128)S(1)} %get-tuple-element.146), kind=kOutput, calls=%fused_computation.13.clone.1 | convolution fusion | flops 541196288 | bytes 9703424 | tf_op jit(solution)/shard_map/while/body/eval_jaxpr/hqk,khe->qhe/dot_general | solution.py:39
  171.9 7.7 %fusion.51 = (f32[2,512]{1,0:T(2,128)S(1)}, f32[2,512,2048]{2,1,0:T(8,128)}) fusion(pred[512,2048]{1,0:T(8,128)(4,1)S(1)} %broadcast_compare_fusion.2, bf16[2048,2,128]{2,0,1:T(8,128)(2,1)} %get-tuple-element.167, bf16[4,512,2,128]{3,1,0,2:T(8,128)(2,1)} %get-tuple-element.166, s32[]{:T(128)} %get-tuple-element.155), kind=kOutput, calls=%fused_computation.56.clone.1 | convolution fusion | flops 545261568 | bytes 10752512 | tf_op jit(solution)/shard_map/while/body/eval_jaxpr/sub | solution.py:20
  179.6 4.7 %fusion.52 = bf16[1,512,2,128]{3,1,2,0:T(8,128)(2,1)S(1)} fusion(bf16[2048,2,128]{2,0,1:T(8,128)(2,1)S(1)} %get-tuple-element.168, f32[2,512,2048]{2,1,0:T(8,128)} %get-tuple-element.145, f32[2,512]{1,0:T(2,128)S(1)} %get-tuple-element.146), kind=kOutput, calls=%fused_computation.13.clone.1 | convolution fusion | flops 541196288 | bytes 9703424 | tf_op jit(solution)/shard_map/while/body/eval_jaxpr/hqk,khe->qhe/dot_general | solution.py:39
  185.3 7.7 %fusion.51 = (f32[2,512]{1,0:T(2,128)S(1)}, f32[2,512,2048]{2,1,0:T(8,128)}) fusion(pred[512,2048]{1,0:T(8,128)(4,1)S(1)} %broadcast_compare_fusion.2, bf16[2048,2,128]{2,0,1:T(8,128)(2,1)} %get-tuple-element.167, bf16[4,512,2,128]{3,1,0,2:T(8,128)(2,1)} %get-tuple-element.166, s32[]{:T(128)} %get-tuple-element.155), kind=kOutput, calls=%fused_computation.56.clone.1 | convolution fusion | flops 545261568 | bytes 10752512 | tf_op jit(solution)/shard_map/while/body/eval_jaxpr/sub | solution.py:20
  193.0 4.7 %fusion.52 = bf16[1,512,2,128]{3,1,2,0:T(8,128)(2,1)S(1)} fusion(bf16[2048,2,128]{2,0,1:T(8,128)(2,1)S(1)} %get-tuple-element.168, f32[2,512,2048]{2,1,0:T(8,128)} %get-tuple-element.145, f32[2,512]{1,0:T(2,128)S(1)} %get-tuple-element.146), kind=kOutput, calls=%fused_computation.13.clone.1 | convolution fusion | flops 541196288 | bytes 9703424 | tf_op jit(solution)/shard_map/while/body/eval_jaxpr/hqk,khe->qhe/dot_general | solution.py:39
  198.0 0.7 all_to_all.28
  198.7 18.5 %all_to_all.34 = bf16[8,256,256]{2,1,0:T(8,128)(2,1)S(1)} all-to-all(bf16[8,256,256]{2,1,0:T(8,128)(2,1)S(1)} %all_to_all.28), channel_id=1, replica_groups=mesh['dp'=64,'ctx'=8] {'ctx'}, dimensions={0} | all-to-all | bytes 2097152 | tf_op jit(solution)/shard_map/all_to_all | solution.py:73
  217.7 46.0 %all-gather.2.cloned.1.call-done = bf16[2048,1536]{1,0:T(8,128)(2,1)} async-done(((bf16[32,1536]{1,0:T(8,128)(2,1)}), bf16[2048,1536]{1,0:T(8,128)(2,1)}) %all-gather.2.cloned.1.call-update) | async-done | bytes 6291472 | tf_op jit(solution)/shard_map/all_gather | solution.py:76
  263.7 5.5 %convolution_convert_fusion = bf16[256,1536]{1,0:T(8,128)(2,1)} fusion(bf16[256,2048]{0,1:T(8,128)(2,1)S(1)} %bitcast.85, bf16[2048,1536]{1,0:T(8,128)(2,1)} %all-gather.2.cloned.1.call-done), kind=kOutput, calls=%fused_computation.29 | convolution fusion | flops 1611005952 | bytes 8126464 | tf_op jit(solution)/shard_map/dot_general | solution.py:74
  (33 shorter events, 7.9 us)
Async XLA Ops:
  6.5 72.1 %collective-permute-start = (bf16[2,128,6144]{2,1,0:T(8,128)(2,1)}, bf16[2,128,6144]{2,1,0:T(8,128)(2,1)S(1)}, u32[]{:S(2)}, u32[]{:S(2)}) collective-permute-start(bf16[2,128,6144]{2,1,0:T(8,128)(2,1)} %bitcast.87), channel_id=1, source_target_pairs={{0,8},{8,0},{16,24},{24,16},{32,40},{40,32},{48,56},{56,48},{64,72... | collective-permute-start | bytes 9437192 | tf_op jit(solution)/shard_map/ppermute | solution.py:14
  99.9 6.3 %copy-start.1 = (s32[1,16]{1,0:T(1,128)S(1)}, s32[1,16]{1,0:T(1,128)}, u32[]{:S(2)}) copy-start(s32[1,16]{1,0:T(1,128)} %param.8) | copy-start | bytes 196
  99.9 42.0 %all-to-all-start = ((bf16[256,8,2,384]{3,2,0,1:T(2,128)(2,1)}), bf16[256,8,2,384]{3,2,0,1:T(2,128)(2,1)S(1)}, u32[]{:S(2)}, u32[]{:S(2)}) async-start(bf16[256,8,2,384]{3,2,0,1:T(2,128)(2,1)} %copy.12), calls=%async_computation | async-start | bytes 6291456 | tf_op jit(solution)/shard_map/all_to_all | solution.py:64
  104.9 158.8 %all-gather.2.cloned.1.call-start = ((), (), s32[]{:S(2)}) async-start(), calls=%async_computation.2 | async-start | bytes 6389760 | tf_op jit(solution)/shard_map/all_gather | solution.py:76
  142.4 1.9 copy-start
Sparse Core Ops, SparseCore 0:
  108.7 155.0 all-gather.1
where the time goes:
time: 277 us; the launch traced here: 276 us
  waiting for transfers between devices  149 us (54%)
  matrix products  54.9 us (20%)
  blocking collectives  18.5 us (7%)
  local copies, waits for them, and re-layouts  17.1 us (6%)
  other arithmetic  14.6 us (5%)
  between operations  13.5 us (5%)
  starting transfers between devices  8.87 us (3%)
    ppermute x1, waiting for transfers between devices, partner(): return lax.ppermute(value, axis, pairs)  66.9 us
    all_gather x1, waiting for transfers between devices, body(): lax.all_gather(out_weight, 'dp', axis=0, tiled=True)  46 us
    all_to_all x1, waiting for transfers between devices, body(): lax.all_to_all(grouped, 'ctx', split_axis=1, concat_axis=0, tiled=True)  35 us
    sub x4, matrix products, soft_weights(): exponent = jnp.exp(masked - row_max)  30.7 us
    dot_general x4, matrix products, one_step(): jnp.einsum('hqk,khe->qhe', weights, value_rows, preferred_element_type=jn...  18.7 us
    all_to_all x1, blocking collectives, body(): lax.all_to_all(merged, 'ctx', split_axis=0, concat_axis=1, tiled=True)  18.5 us
    gather x2, local copies, waits for them, and re-layouts, body(): packed = jnp.take(candidates, chosen_slot, axis=0)  7.07 us
    select_n x2, other arithmetic, body(): packed = jnp.take(candidates, chosen_slot, axis=0)  5.63 us
  transfers between devices with their start and end apart: 3, of which 3 were waited for; matrix products, arithmetic and copies ran while one was open for 21% of the time, Pallas kernels for 0%

commit v1 on v0

--- a/solution.py
+++ b/solution.py
@@ -71,10 +71,14 @@
     attended = attend_dense(queries, key_rows, value_rows, token_clip, scaling)
     merged = attended.reshape(local_rows * ctx_count, local_heads * HEAD)
     attention_rows = lax.all_to_all(merged, "ctx", split_axis=0, concat_axis=1, tiled=True)
+    _supply_shifts_all = lambda t0, shard_axis: jnp.concatenate(
+        lax.all_to_all(
+            jnp.stack([t0 for _ in range(lax.axis_size(shard_axis))], 0), shard_axis, 0, 0
+        ),
+        0,
+    )
     result = jnp.dot(
-        attention_rows,
-        lax.all_gather(out_weight, "dp", axis=0, tiled=True),
-        preferred_element_type=jnp.float32,
+        attention_rows, _supply_shifts_all(out_weight, "dp"), preferred_element_type=jnp.float32
     )
     return result.astype(jnp.bfloat16)
 

time: 277 us -> 517 us (1.87)
  waiting for transfers between devices: 149 us -> 380 us
  starting transfers between devices: 8.87 us -> 27.3 us
  between operations: 13.5 us -> 0.1 us
    all_to_all x0 -> x1, waiting for transfers between devices: none -> 278 us  [body(): lax.all_to_all(jnp.stack([t0 for _ in range(lax.axis_size(shard_axis))],...]
    all_gather x1 -> x0, waiting for transfers between devices: 46 us -> none  [body(): lax.all_gather(out_weight, 'dp', axis=0, tiled=True)]
    all_to_all x0 -> x1, starting transfers between devices: none -> 18.6 us  [body(): lax.all_to_all(jnp.stack([t0 for _ in range(lax.axis_size(shard_axis))],...]
  transfers between devices with their start and end apart: 3 -> 3, of which waited for: 3 -> 3; matrix products, arithmetic and copies ran while one was open for 21% -> 1% of each run, Pallas kernels for 0% -> 0%
where the time goes in v1:
time: 517 us; the launch traced here: 516 us
  waiting for transfers between devices  380 us (74%)
  matrix products  54.9 us (11%)
  starting transfers between devices  27.3 us (5%)
  local copies, waits for them, and re-layouts  20.5 us (4%)
  blocking collectives  18.5 us (4%)
  other arithmetic  14.6 us (3%)
    all_to_all x1, waiting for transfers between devices, body(): lax.all_to_all(jnp.stack([t0 for _ in range(lax.axis_size(shard_axis))],...  278 us
    ppermute x1, waiting for transfers between devices, partner(): return lax.ppermute(value, axis, pairs)  66.9 us
    all_to_all x1, waiting for transfers between devices, body(): lax.all_to_all(grouped, 'ctx', split_axis=1, concat_axis=0, tiled=True)  35.7 us
    sub x4, matrix products, soft_weights(): exponent = jnp.exp(masked - row_max)  30.7 us
    dot_general x4, matrix products, one_step(): jnp.einsum('hqk,khe->qhe', weights, value_rows, preferred_element_type=jn...  18.7 us
    all_to_all x1, starting transfers between devices, body(): lax.all_to_all(jnp.stack([t0 for _ in range(lax.axis_size(shard_axis))],...  18.6 us
    all_to_all x1, blocking collectives, body(): lax.all_to_all(merged, 'ctx', split_axis=0, concat_axis=1, tiled=True)  18.5 us
  transfers between devices with their start and end apart: 3, of which 3 were waited for; matrix products, arithmetic and copies ran while one was open for 1% of the time, Pallas kernels for 0%

profile of v1, /device:TPU:8, one launch (start us, length us, event | category | flops | bytes accessed | tf_op | source)
XLA Modules:
  0.0 516.5 jit_solution(18226603314352265200)
XLA Ops:
  0.0 3.8 collective-permute-start
  5.3 66.9 %collective-permute-done = bf16[2,128,6144]{2,1,0:T(8,128)(2,1)S(1)} collective-permute-done((bf16[2,128,6144]{2,1,0:T(8,128)(2,1)}, bf16[2,128,6144]{2,1,0:T(8,128)(2,1)S(1)}, u32[]{:S(2)}, u32[]{:S(2)}) %collective-permute-start) | collective-permute-done | bytes 3145760 | tf_op jit(solution)/shard_map/ppermute | solution.py:14
  72.1 5.1 pad_maximum_fusion
  77.2 3.5 gather_fusion
  80.7 3.5 gather.7
  84.3 5.0 broadcast_select_fusion
  89.3 4.1 copy.12
  93.3 4.9 all-to-all-start
  99.5 35.7 %all-to-all-done = bf16[256,8,2,384]{3,2,0,1:T(2,128)(2,1)S(1)} async-done(((bf16[256,8,2,384]{3,2,0,1:T(2,128)(2,1)}), bf16[256,8,2,384]{3,2,0,1:T(2,128)(2,1)S(1)}, u32[]{:S(2)}, u32[]{:S(2)}) %all-to-all-start) | async-done | bytes 3145760 | tf_op jit(solution)/shard_map/all_to_all | solution.py:64
  135.8 1.9 fusion.37
  137.7 53.6 %while.11 = (s32[]{:T(128)}, bf16[4,512,2,128]{3,2,1,0:T(2,128)(2,1)S(1)}, s32[4,512]{1,0:T(4,128)S(1)}, bf16[4,512,2,128]{3,1,0,2:T(8,128)(2,1)}, bf16[2048,2,1...) while((s32[]{:T(128)}, ...), condition=%wide.region_3.4_spmd.clone, body=%wide.region_0.3_spmd.clone.sunk | while | flops 1087506432 | bytes 22051484 | solution.py:43
  138.5 7.7 %fusion.51 = (f32[2,512]{1,0:T(2,128)S(1)}, f32[2,512,2048]{2,1,0:T(8,128)}) fusion(pred[512,2048]{1,0:T(8,128)(4,1)S(1)} %broadcast_compare_fusion.2, bf16[2048,2,128]{2,0,1:T(8,128)(2,1)} %get-tuple-element.167, bf16[4,512,2,128]{3,1,0,2:T(8,128)(2,1)} %get-tuple-element.166, s32[]{:T(128)} %get-tuple-element.155), kind=kOutput, calls=%fused_computation.56.clone.1 | convolution fusion | flops 545261568 | bytes 10752512 | tf_op jit(solution)/shard_map/while/body/eval_jaxpr/sub | solution.py:20
  146.1 4.7 fusion.52
  151.9 7.7 %fusion.51 = (f32[2,512]{1,0:T(2,128)S(1)}, f32[2,512,2048]{2,1,0:T(8,128)}) fusion(pred[512,2048]{1,0:T(8,128)(4,1)S(1)} %broadcast_compare_fusion.2, bf16[2048,2,128]{2,0,1:T(8,128)(2,1)} %get-tuple-element.167, bf16[4,512,2,128]{3,1,0,2:T(8,128)(2,1)} %get-tuple-element.166, s32[]{:T(128)} %get-tuple-element.155), kind=kOutput, calls=%fused_computation.56.clone.1 | convolution fusion | flops 545261568 | bytes 10752512 | tf_op jit(solution)/shard_map/while/body/eval_jaxpr/sub | solution.py:20
  159.5 4.7 fusion.52
  165.3 7.7 %fusion.51 = (f32[2,512]{1,0:T(2,128)S(1)}, f32[2,512,2048]{2,1,0:T(8,128)}) fusion(pred[512,2048]{1,0:T(8,128)(4,1)S(1)} %broadcast_compare_fusion.2, bf16[2048,2,128]{2,0,1:T(8,128)(2,1)} %get-tuple-element.167, bf16[4,512,2,128]{3,1,0,2:T(8,128)(2,1)} %get-tuple-element.166, s32[]{:T(128)} %get-tuple-element.155), kind=kOutput, calls=%fused_computation.56.clone.1 | convolution fusion | flops 545261568 | bytes 10752512 | tf_op jit(solution)/shard_map/while/body/eval_jaxpr/sub | solution.py:20
  173.0 4.7 fusion.52
  178.7 7.7 %fusion.51 = (f32[2,512]{1,0:T(2,128)S(1)}, f32[2,512,2048]{2,1,0:T(8,128)}) fusion(pred[512,2048]{1,0:T(8,128)(4,1)S(1)} %broadcast_compare_fusion.2, bf16[2048,2,128]{2,0,1:T(8,128)(2,1)} %get-tuple-element.167, bf16[4,512,2,128]{3,1,0,2:T(8,128)(2,1)} %get-tuple-element.166, s32[]{:T(128)} %get-tuple-element.155), kind=kOutput, calls=%fused_computation.56.clone.1 | convolution fusion | flops 545261568 | bytes 10752512 | tf_op jit(solution)/shard_map/while/body/eval_jaxpr/sub | solution.py:20
  186.4 4.7 fusion.52
  192.1 18.5 %all_to_all.39 = bf16[8,256,256]{2,1,0:T(8,128)(2,1)S(1)} all-to-all(bf16[8,256,256]{2,1,0:T(8,128)(2,1)S(1)} %all_to_all.31), channel_id=1, replica_groups=mesh['dp'=64,'ctx'=8] {'ctx'}, dimensions={0} | all-to-all | bytes 2097152 | tf_op jit(solution)/shard_map/all_to_all | solution.py:73
  210.6 3.4 stack.2
  214.0 18.6 %all-to-all-start.2 = ((bf16[64,32,1536]{2,1,0:T(8,128)(2,1)}), bf16[64,32,1536]{2,1,0:T(8,128)(2,1)}, u32[]{:S(2)}, u32[]{:S(2)}) async-start(bf16[64,32,1536]{2,1,0:T(8,128)(2,1)} %stack.2), calls=%async_computation.2 | async-start | bytes 12582912 | tf_op jit(solution)/shard_map/all_to_all | solution.py:75
  233.1 277.9 %all-to-all-done.2 = bf16[64,32,1536]{2,1,0:T(8,128)(2,1)} async-done(((bf16[64,32,1536]{2,1,0:T(8,128)(2,1)}), bf16[64,32,1536]{2,1,0:T(8,128)(2,1)}, u32[]{:S(2)}, u32[]{:S(2)}) %all-to-all-start.2) | async-done | bytes 6291488 | tf_op jit(solution)/shard_map/all_to_all | solution.py:75
  511.0 5.5 %convolution_convert_fusion = bf16[256,1536]{1,0:T(8,128)(2,1)} fusion(bf16[256,2048]{0,1:T(8,128)(2,1)S(1)} %bitcast.86, bf16[2048,1536]{1,0:T(8,128)(2,1)} %bitcast.14), kind=kOutput, calls=%fused_computation.29 | convolution fusion | flops 1611005952 | bytes 8126464 | tf_op jit(solution)/shard_map/dot_general | solution.py:80
  (35 shorter events, 8.6 us)
Async XLA Ops:
  0.0 72.1 %collective-permute-start = (bf16[2,128,6144]{2,1,0:T(8,128)(2,1)}, bf16[2,128,6144]{2,1,0:T(8,128)(2,1)S(1)}, u32[]{:S(2)}, u32[]{:S(2)}) collective-permute-start(bf16[2,128,6144]{2,1,0:T(8,128)(2,1)} %bitcast.88), channel_id=1, source_target_pairs={{0,8},{8,0},{16,24},{24,16},{32,40},{40,32},{48,56},{56,48},{64,72... | collective-permute-start | bytes 9437192 | tf_op jit(solution)/shard_map/ppermute | solution.py:14
  89.2 9.5 %copy-start.2 = (s32[1,16]{1,0:T(1,128)S(1)}, s32[1,16]{1,0:T(1,128)}, u32[]{:S(2)}) copy-start(s32[1,16]{1,0:T(1,128)} %param.8) | copy-start | bytes 196
  93.3 41.9 %all-to-all-start = ((bf16[256,8,2,384]{3,2,0,1:T(2,128)(2,1)}), bf16[256,8,2,384]{3,2,0,1:T(2,128)(2,1)S(1)}, u32[]{:S(2)}, u32[]{:S(2)}) async-start(bf16[256,8,2,384]{3,2,0,1:T(2,128)(2,1)} %copy.12), calls=%async_computation | async-start | bytes 6291456 | tf_op jit(solution)/shard_map/all_to_all | solution.py:64
  135.8 1.9 copy-start
  137.7 72.8 %copy-start.1 = (bf16[32,1536]{1,0:T(8,128)(2,1)S(1)}, bf16[32,1536]{1,0:T(8,128)(2,1)}, u32[]{:S(2)}) copy-start(bf16[32,1536]{1,0:T(8,128)(2,1)} %param.9) | copy-start | bytes 294916
  214.0 297.0 %all-to-all-start.2 = ((bf16[64,32,1536]{2,1,0:T(8,128)(2,1)}), bf16[64,32,1536]{2,1,0:T(8,128)(2,1)}, u32[]{:S(2)}, u32[]{:S(2)}) async-start(bf16[64,32,1536]{2,1,0:T(8,128)(2,1)} %stack.2), calls=%async_computation.2 | async-start | bytes 12582912 | tf_op jit(solution)/shard_map/all_to_all | solution.py:75
